TPU v7x, 128 devices: a whole 4x4x4 slice. The times are simulated.
128 devices in a mesh: gx: 16 (over x, y), gy: 8 (over z, core).
Axes of the slice: x: 4, y: 4, z: 4, core: 2. Of those that a mesh axis runs over, the one named last changes fastest.
Arguments:
- estimate: float32 [32, 256, 1024], P(None, 'gx', 'gy'), may hold values from 0.5 to 2
- stored: bfloat16 [16384, 16, 128], P(('gx', 'gy')), may hold values from 0.19921875 to 5
- placement: int32 [16384], replicated, may hold values from 0 to 16383, as said below
- psf_taps: float32 [48, 31], replicated, may hold values from 0.05 to 1
- kernel_index: int32 [16, 8, 4, 3], replicated, may hold values from 0 to 47
Outputs:
- refined: float32 [32, 256, 1024], P(None, 'gx', 'gy')
Inputs may be any that keep to these rules, and one draw needn't show every extreme that they name: `placement`: each value occurs once; the value b * 128 + v * 32 + z marks plane z of view v of brick b. Entries d * 128 to (d + 1) * 128 - 1 are the slots of device d of gx+gy; among them at most 2 name any one brick, every device has exactly 2 naming some brick, and every brick has exactly 2 on some device.
All inputs are finite; a program needn't handle non-finite values.
Results may differ from a plain program's by a relative error of at most 0.0003.
Values may be sent and summed in bfloat16 or wider, within the bound.
A program may use at most 128 MiB of HBM per device.

v0:
```python
import functools

import jax
import jax.numpy as jnp
from jax import lax
from jax.experimental import pallas as pl
from jax.experimental.pallas import tpu as pltpu
from jax.sharding import PartitionSpec as P

ITERS = 2
MESH = pl.DeviceIdType.MESH
F32 = jnp.float32
BF16 = jnp.bfloat16


def dot(a, b):
    return jnp.dot(a, b, preferred_element_type=F32)


def dot_nt(a, b):
    return lax.dot_general(a, b, (((1,), (1,)), ((), ())), preferred_element_type=F32)


def iota(shape, dim):
    return lax.broadcasted_iota(jnp.int32, shape, dim)


def deblur_kernel(
    devices_x, devices_y, planes, ext_x, views,
    est_ref, arrived_ref, rows_ref, kidx_ref, psf_ref, out_ref,
    table, kz_small, kx_small, kz_wide, kx_wide, wy, kf, kt,
    cur, cbuf, zcat, blur, rim, rim_send, rim_recv, qext, q_send, q_recv, u, part, part_recv, meas,
    send_sem, recv_sem,
):
    zx = planes * ext_x
    ny = est_ref.shape[1]
    taps = psf_ref.shape[1]
    rad = (taps - 1) // 2
    half = zx // 2
    gx = lax.axis_index("gx")
    gy = lax.axis_index("gy")
    has = {
        "left": gx > 0,
        "right": gx < devices_x - 1,
        "down": gy > 0,
        "up": gy < devices_y - 1,
    }
    to = {
        "left": (gx - 1, gy),
        "right": (gx + 1, gy),
        "down": (gx, gy - 1),
        "up": (gx, gy + 1),
    }
    slot_of = {"left": 0, "right": 1, "down": 0, "up": 1}
    back = {"left": "right", "right": "left", "down": "up", "up": "down"}

    barrier = pltpu.get_barrier_semaphore()
    for side in has:
        @pl.when(has[side])
        def _(side=side):
            pl.semaphore_signal(barrier, inc=1, device_id=to[side], device_id_type=MESH)

    def send(side, kind, src, dst):
        num = kind * 2 + slot_of[side]

        @pl.when(has[side])
        def _():
            pltpu.make_async_remote_copy(
                src_ref=src, dst_ref=dst, send_sem=send_sem.at[num],
                recv_sem=recv_sem.at[kind * 2 + slot_of[side]],
                device_id=to[side], device_id_type=MESH,
            ).start()

    def wait_send(side, kind, src):
        num = kind * 2 + slot_of[side]

        @pl.when(has[side])
        def _():
            pltpu.make_async_remote_copy(
                src_ref=src, dst_ref=src, send_sem=send_sem.at[num], recv_sem=recv_sem.at[num],
                device_id=to[side], device_id_type=MESH,
            ).wait_send()

    def wait_recv(side, kind, dst):
        num = kind * 2 + slot_of[back[side]]

        @pl.when(has[side])
        def _():
            pltpu.make_async_remote_copy(
                src_ref=dst, dst_ref=dst, send_sem=send_sem.at[num], recv_sem=recv_sem.at[num],
                device_id=to[side], device_id_type=MESH,
            ).wait_recv()

    def clear_missing(side, dst):
        @pl.when(jnp.logical_not(has[side]))
        def _():
            dst[...] = jnp.zeros(dst.shape, dst.dtype)

    cur[...] = est_ref[...]
    cbuf[0, 1] = cur[...].astype(BF16)
    for it in range(ITERS):
        clear_missing("left", cbuf.at[it, 0])
        clear_missing("right", cbuf.at[it, 2])
        for kind_buf in (rim_recv, q_recv):
            clear_missing("down", kind_buf.at[it, 0])
            clear_missing("up", kind_buf.at[it, 1])
        clear_missing("left", part_recv.at[it, 0])
        clear_missing("right", part_recv.at[it, 1])
    peers = sum(present.astype(jnp.int32) for present in has.values())
    pl.semaphore_wait(barrier, peers)

    def send_current(it):
        send("left", 4 * it, cbuf.at[it, 1], cbuf.at[it, 2])
        send("right", 4 * it, cbuf.at[it, 1], cbuf.at[it, 0])

    send_current(0)

    weights = psf_ref[...]
    weights = weights / jnp.sum(weights, axis=1, keepdims=True)
    tap = iota((taps, 128), 0)
    lane = iota((taps, 128), 1)

    def spread_taps(distance):
        select = (lane == jnp.where(distance < 0, distance + 128, distance)).astype(F32)
        return jnp.dot(weights, select, precision=lax.Precision.HIGHEST, preferred_element_type=F32)

    blocks = [tap - rad, rad - tap]
    blocks += [tap - rad - o for o in (-ext_x, 0, ext_x)]
    blocks += [rad + o - tap for o in (-ext_x, 0, ext_x)]
    for num, distance in enumerate(blocks):
        table[num] = spread_taps(distance)
    rounded = table[1].astype(BF16).astype(F32)
    scale = 1.0 / jnp.sum(rounded, axis=1, keepdims=True)
    table[8] = jnp.broadcast_to(scale, (scale.shape[0], 128))

    def toeplitz(base, count):
        return pltpu.roll(jnp.broadcast_to(base, (count, 128)), 0, 1, stride=1, stride_axis=0)

    def two_parts(matrix, width):
        where = iota(matrix.shape, 1)
        low = matrix - matrix.astype(BF16).astype(F32)
        return jnp.where(where < width, matrix, pltpu.roll(low, width, 1)).astype(BF16)

    for i in range(3):
        brick_x = jnp.clip(gx + (i - 1), 0, devices_x - 1)
        for v in range(views):
            n = i * views + v
            first = ((brick_x * devices_y + gy) * views + v) * 3
            id_x, id_y, id_z = (kidx_ref[first + e] for e in range(3))
            factor = table[8, pl.ds(id_y, 1), :]
            for way in range(2):
                base = table[way, pl.ds(id_z, 1), :] * factor
                at = (way * 3 * views + n) * planes
                kz_small[at:at + planes, :] = two_parts(toeplitz(base, planes), planes)
                block = 2 + 3 * way + i
                base = table[block, pl.ds(id_x, 1), :]
                at = (way * 3 * views + n) * ext_x
                kx_small[at:at + ext_x, :] = two_parts(toeplitz(base, ext_x), ext_x)
            ring = toeplitz(table[1, pl.ds(id_y, 1), :], ny)
            apart = iota((ny, 128), 1) - iota((ny, 128), 0)
            near = (apart >= -rad) & (apart <= rad)
            wy[v, i * ny:(i + 1) * ny, 0:128] = jnp.where(near, ring, 0.0).astype(BF16)
            edge = jnp.where(near, 0.0, ring)
            if v:
                edge = pltpu.roll(edge, 32 * v, 1)
            wy[v, i * ny:(i + 1) * ny, 128:256] = edge.astype(BF16)

    wide = (128, zx)
    row = iota(wide, 0)
    col = iota(wide, 1)
    col_z = col // ext_x
    col_x = lax.rem(col, ext_x)
    pick_z = ((row == col_z) | (row == col_z + planes)).astype(F32).astype(BF16)
    pick_x = ((row == col_x) | (row == col_x + ext_x)).astype(F32).astype(BF16)

    def expand(n, carry):
        at = pl.multiple_of(n * 96, 32)
        res = dot(kz_small[pl.ds(at, 96), :], pick_z)
        for part_num in range(zx // 128):
            kz_wide[part_num, pl.ds(at, 96), :] = res[:, part_num * 128:(part_num + 1) * 128]
        return carry

    lax.fori_loop(0, kz_small.shape[0] // 96, expand, 0)
    kx_wide[...] = dot(kx_small[...], pick_x[:, 0:128])

    def build(way):
        def one(n, carry):
            i = n // views
            v = lax.rem(n, views)
            num = way * 3 * views + n
            tile = kx_wide[pl.ds(pl.multiple_of(num * ext_x, 16), ext_x), :]
            for z in range(planes):
                for b in range(zx // 128):
                    line = kz_wide[b, pl.ds(num * planes + z, 1), :]
                    value = (jnp.broadcast_to(line, (ext_x, 128)) * tile).astype(BF16)
                    if way == 0:
                        at = pl.multiple_of(v * zx + z * ext_x, 16)
                        kf[i, pl.ds(at, ext_x), b * 128:(b + 1) * 128] = value
                    else:
                        at = pl.multiple_of(v * zx + b * 128, 128)
                        kt[i, z * ext_x:(z + 1) * ext_x, pl.ds(at, 128)] = value
            return carry

        lax.fori_loop(0, 3 * views, one, 0)

    build(0)

    lane_half = iota((half, 128), 1)
    low_half = lax.rem(lane_half, 32) < 16

    def fold(value, first):
        top, bottom = value[0:half], value[half:zx]
        if first:
            return jnp.where(low_half, top, pltpu.roll(bottom, 16, 1)).astype(BF16)
        return jnp.where(low_half, pltpu.roll(bottom, 112, 1), top).astype(BF16)

    def unfold(from_first, from_second):
        a, b = from_first.astype(F32), from_second.astype(F32)
        top = jnp.where(low_half, a, b)
        bottom = jnp.where(low_half, pltpu.roll(a, 112, 1), pltpu.roll(b, 16, 1))
        return top, bottom

    def forward_zx(it, i):
        def one(v, carry):
            at = pl.multiple_of(v * zx, zx)
            zcat[pl.ds(at, zx), i * ny:(i + 1) * ny] = dot(
                kf[i, pl.ds(at, zx), :], cbuf[it, i]
            ).astype(BF16)
            return carry

        lax.fori_loop(0, views, one, 0)

    def forward_y():
        rim[...] = jnp.zeros(rim.shape, F32)

        def one(v, carry):
            at = pl.multiple_of(v * zx, zx)
            res = dot(zcat[pl.ds(at, zx), :], wy[v])
            blur[pl.ds(at, zx), :] = res[:, 0:128]
            rim[...] += res[:, 128:256]
            return carry

        lax.fori_loop(0, views, one, 0)

    def adjoint_y():
        def one(v, carry):
            at = pl.multiple_of(v * zx, zx)
            res = dot_nt(qext[pl.ds(at, zx), :], wy[v]).astype(BF16)
            for i in range(3):
                u[i, pl.ds(at, zx), :] = res[:, i * ny:(i + 1) * ny]
            return carry

        lax.fori_loop(0, views, one, 0)

    lane_q = iota((zx, 128), 1)
    low_q = lax.rem(lane_q, 32) < 16

    for it in range(ITERS):
        kind_c, kind_rim, kind_q, kind_p = (4 * it + k for k in range(4))
        forward_zx(it, 1)
        wait_recv("left", kind_c, cbuf.at[it, 0])
        wait_recv("right", kind_c, cbuf.at[it, 2])
        forward_zx(it, 0)
        forward_zx(it, 2)
        forward_y()
        rim_send[it, 1] = fold(rim[...], True)
        rim_send[it, 0] = fold(rim[...], False)
        send("up", kind_rim, rim_send.at[it, 1], rim_recv.at[it, 0])
        send("down", kind_rim, rim_send.at[it, 0], rim_recv.at[it, 1])
        if it == 0:
            build(1)

            def take(p, carry):
                meas[pl.ds(pl.multiple_of(p * ext_x, ext_x), ext_x), :] = arrived_ref[rows_ref[p]]
                return carry

            lax.fori_loop(0, views * planes, take, 0)
        wait_recv("down", kind_rim, rim_recv.at[it, 0])
        wait_recv("up", kind_rim, rim_recv.at[it, 1])
        tops = unfold(rim_recv[it, 0], rim_recv[it, 1])
        rim[0:half] = tops[0]
        rim[half:zx] = tops[1]
        packed = jnp.zeros((zx, 128), F32)
        for v in range(views):
            add = rim[...]
            if v:
                add = pltpu.roll(add, 128 - 32 * v, 1)
            edge = (lane_q < rad) | (lane_q >= 128 - rad)
            total = blur[v * zx:(v + 1) * zx, :] + jnp.where(edge, add, 0.0)
            q = meas[v * zx:(v + 1) * zx, :].astype(F32) / total
            qext[v * zx:(v + 1) * zx, 0:128] = q.astype(BF16)
            moved = pltpu.roll(q, 32 * v, 1) if v else q
            place = lax.rem(lane_q - 32 * v + 128 + rad, 128)
            packed = jnp.where(place < 2 * rad, moved, packed)
        q_send[it, 0] = fold(packed, True)
        q_send[it, 1] = fold(packed, False)
        send("down", kind_q, q_send.at[it, 0], q_recv.at[it, 1])
        send("up", kind_q, q_send.at[it, 1], q_recv.at[it, 0])
        wait_recv("down", kind_q, q_recv.at[it, 0])
        wait_recv("up", kind_q, q_recv.at[it, 1])
        tops = unfold(q_recv[it, 1], q_recv[it, 0])
        for v in range(views):
            qext[v * zx:v * zx + half, 128:256] = tops[0].astype(BF16)
            qext[v * zx + half:(v + 1) * zx, 128:256] = tops[1].astype(BF16)
        adjoint_y()
        part[it, 0] = dot(kt[0], u[0])
        send("left", kind_p, part.at[it, 0], part_recv.at[it, 1])
        part[it, 1] = dot(kt[2], u[2])
        send("right", kind_p, part.at[it, 1], part_recv.at[it, 0])
        own = dot(kt[1], u[1])
        wait_recv("left", kind_p, part_recv.at[it, 0])
        wait_recv("right", kind_p, part_recv.at[it, 1])
        correction = (own + part_recv[it, 0] + part_recv[it, 1]) * (1.0 / views)
        updated = cur[...] * correction
        if it < ITERS - 1:
            cur[...] = updated
            cbuf[it + 1, 1] = updated.astype(BF16)
            send_current(it + 1)
        else:
            out_ref[...] = updated

    for it in range(ITERS):
        kind_c, kind_rim, kind_q, kind_p = (4 * it + k for k in range(4))
        for side in ("left", "right"):
            wait_send(side, kind_c, cbuf.at[it, 1])
            wait_send(side, kind_p, part.at[it, 0])
        for side in ("down", "up"):
            wait_send(side, kind_rim, rim_send.at[it, 0])
            wait_send(side, kind_q, q_send.at[it, 0])


def exchange(stored, placement, devices):
    slots = stored.shape[0]
    me = lax.axis_index("gx") * lax.axis_size("gy") + lax.axis_index("gy")
    slot = jnp.arange(slots, dtype=jnp.int32)[None, :]
    own = lax.dynamic_slice_in_dim(placement, me * slots, slots) // slots
    match = own[None, :] == jnp.arange(devices, dtype=jnp.int32)[:, None]
    first = jnp.min(jnp.where(match, slot, slots - 1), axis=1)
    last = jnp.max(jnp.where(match, slot, 0), axis=1)
    source = jnp.stack([first, last], axis=1).reshape(-1)
    outgoing = jnp.take(stored, source, axis=0, mode="clip")
    outgoing = outgoing.reshape((devices, 2) + stored.shape[1:])
    arrived = lax.all_to_all(outgoing, ("gx", "gy"), split_axis=0, concat_axis=0, tiled=True)
    everything = placement.reshape(devices, slots)
    wanted = everything // slots == me
    item = everything % slots
    first = jnp.min(jnp.where(wanted, slot, slots), axis=1, keepdims=True)
    last = jnp.max(jnp.where(wanted, slot, -1), axis=1, keepdims=True)
    item_first = jnp.max(jnp.where(slot == first, item, -1), axis=1)
    item_last = jnp.max(jnp.where((slot == last) & (last > first), item, -1), axis=1)
    items = jnp.arange(slots, dtype=jnp.int32)[:, None]
    origin = jnp.arange(devices, dtype=jnp.int32)[None, :]
    row = jnp.max(
        jnp.where(item_first[None, :] == items, 2 * origin, 0)
        + jnp.where(item_last[None, :] == items, 2 * origin + 1, 0),
        axis=1,
    )
    return arrived.reshape((2 * devices,) + stored.shape[1:]), row


def solution(mesh):
    devices_x, devices_y = mesh.shape["gx"], mesh.shape["gy"]

    def shards(estimate, stored, placement, psf_taps, kernel_index):
        planes, ext_x, ny = estimate.shape
        zx = planes * ext_x
        views = kernel_index.shape[2]
        arrived, row = exchange(stored, placement, devices_x * devices_y)
        vmem = pl.BlockSpec(memory_space=pltpu.VMEM)
        smem = pl.BlockSpec(memory_space=pltpu.SMEM)
        n = 3 * views
        half = zx // 2
        refined = pl.pallas_call(
            functools.partial(deblur_kernel, devices_x, devices_y, planes, ext_x, views),
            out_shape=jax.ShapeDtypeStruct((zx, ny), F32),
            in_specs=[vmem, vmem, smem, smem, vmem],
            out_specs=vmem,
            scratch_shapes=[
                pltpu.VMEM((9, psf_taps.shape[0], 128), F32),
                pltpu.VMEM((2 * n * planes, 128), BF16),
                pltpu.VMEM((2 * n * ext_x, 128), BF16),
                pltpu.VMEM((zx // 128, 2 * n * planes, 128), F32),
                pltpu.VMEM((2 * n * ext_x, 128), F32),
                pltpu.VMEM((views, 3 * ny, 256), BF16),
                pltpu.VMEM((3, views * zx, zx), BF16),
                pltpu.VMEM((3, zx, views * zx), BF16),
                pltpu.VMEM((zx, ny), F32),
                pltpu.VMEM((ITERS, 3, zx, ny), BF16),
                pltpu.VMEM((views * zx, 3 * ny), BF16),
                pltpu.VMEM((views * zx, ny), F32),
                pltpu.VMEM((zx, 128), F32),
                pltpu.VMEM((ITERS, 2, half, 128), BF16),
                pltpu.VMEM((ITERS, 2, half, 128), BF16),
                pltpu.VMEM((views * zx, 256), BF16),
                pltpu.VMEM((ITERS, 2, half, 128), BF16),
                pltpu.VMEM((ITERS, 2, half, 128), BF16),
                pltpu.VMEM((3, views * zx, ny), BF16),
                pltpu.VMEM((ITERS, 2, zx, ny), F32),
                pltpu.VMEM((ITERS, 2, zx, ny), F32),
                pltpu.VMEM((views * zx, ny), BF16),
                pltpu.SemaphoreType.DMA((8 * ITERS,)),
                pltpu.SemaphoreType.DMA((8 * ITERS,)),
            ],
            compiler_params=pltpu.CompilerParams(
                collective_id=0, has_side_effects=True, vmem_limit_bytes=60 * 1024 * 1024
            ),
        )(
            estimate.reshape(zx, ny),
            arrived,
            row,
            kernel_index.reshape(-1),
            psf_taps,
        )
        return refined.reshape(planes, ext_x, ny)

    return jax.shard_map(
        shards,
        mesh=mesh,
        in_specs=(P(None, "gx", "gy"), P(("gx", "gy"), None, None), P(), P(), P()),
        out_specs=P(None, "gx", "gy"),
        check_vma=False,
    )
```

profile of v0, /device:TPU:3, one launch (start us, length us, event | category | flops | bytes accessed | tf_op | source)
XLA Modules:
  0.0 93.1 jit_solution(17914195590461655865)
XLA Ops:
  0.0 0.0 copy-start
  0.0 0.8 and_select_fusion
  0.8 0.1 select_reduce_fusion.5
  1.0 0.1 copy.10
  1.1 0.1 reshape.47
  1.2 0.0 copy-done
  1.2 1.8 %gather_fusion = bf16[256,16,128]{2,1,0:T(8,128)(2,1)} fusion(bf16[128,16,128]{2,1,0:T(8,128)(2,1)S(1)} %copy-done, s32[1024]{0:T(1024)S(1)} %pad_clamp_fusion), kind=kCustom, calls=%fused_computation | custom fusion | bytes 2098176 | tf_op jit(solution)/shard_map/jit(_take)/gather | solution.py:341
  3.0 0.0 copy-start.3
  3.0 10.8 %all-to-all-start = ((bf16[128,2,16,128]{3,2,1,0:T(8,128)(2,1)}), bf16[128,2,16,128]{3,2,1,0:T(8,128)(2,1)S(1)}, u32[]{:S(2)}, u32[]{:S(2)}) async-start(bf16[128,2,16,128]{3,2,1,0:T(8,128)(2,1)} %bitcast.3), calls=%async_computation | async-start | bytes 2097152 | tf_op jit(solution)/shard_map/all_to_all | solution.py:343
  13.9 0.0 copy-done.3
  13.9 0.4 copy.11
  14.3 0.0 copy-start.4
  14.3 0.0 copy-start.2
  14.3 0.9 reshape.43.kidx_ref
  15.2 0.0 copy-done.4
  15.2 0.7 copy.12.psf_ref
  15.9 0.0 copy-done.2
  15.9 0.1 select_reduce_fusion.3
  16.0 0.2 select_reduce_fusion.2
  16.2 0.6 add_reduce_fusion.rows_ref
  16.9 15.2 %all-to-all-done = bf16[128,2,16,128]{3,2,1,0:T(8,128)(2,1)S(1)} async-done(((bf16[128,2,16,128]{3,2,1,0:T(8,128)(2,1)}), bf16[128,2,16,128]{3,2,1,0:T(8,128)(2,1)S(1)}, u32[]{:S(2)}, u32[]{:S(2)}) %all-to-all-start) | async-done | bytes 1048608 | tf_op jit(solution)/shard_map/all_to_all | solution.py:343
  32.1 0.0 copy-start.1
  32.1 1.0 %copy-done.1 = bf16[128,2,16,128]{3,2,1,0:T(8,128)(2,1)} copy-done((bf16[128,2,16,128]{3,2,1,0:T(8,128)(2,1)}, bf16[128,2,16,128]{3,2,1,0:T(8,128)(2,1)S(1)}, u32[]{:S(2)}) %copy-start.1) | copy-done | bytes 1048600
  33.0 58.4 %shard_map.55 = f32[512,128]{1,0:T(8,128)} custom-call(f32[512,128]{1,0:T(8,128)} %bitcast.38, bf16[256,16,128]{2,1,0:T(8,128)(2,1)} %bitcast.36, s32[128]{0:T(128)} %add_reduce_fusion.rows_ref, s32[1536]{0:T(1024)} %reshape.43.kidx_ref, f32[48,31]{1,0:T(8,128)} %copy.12.psf_ref), custom_call_target="tpu_custom_call" | custom-call | tf_op jit(solution)/shard_map/pallas_call | solution.py:373
  91.5 1.7 %copy.14 = f32[32,16,128]{2,1,0:T(8,128)} copy(f32[32,16,128]{2,1,0:T(8,128)} %bitcast.37) | data formatting | bytes 524288
  (4 shorter events, 0.0 us)
Async XLA Ops:
  0.0 1.2 %copy-start = (bf16[128,16,128]{2,1,0:T(8,128)(2,1)S(1)}, bf16[128,16,128]{2,1,0:T(8,128)(2,1)}, u32[]{:S(2)}) copy-start(bf16[128,16,128]{2,1,0:T(8,128)(2,1)} %param.6) | copy-start | bytes 1572868
  3.0 10.9 %copy-start.3 = (s32[16,8,4,3]{0,2,3,1:T(4,128)S(1)}, s32[16,8,4,3]{0,2,3,1:T(4,128)}, u32[]{:S(2)}) copy-start(s32[16,8,4,3]{0,2,3,1:T(4,128)} %param.9) | copy-start | bytes 18436
  3.0 29.0 %all-to-all-start = ((bf16[128,2,16,128]{3,2,1,0:T(8,128)(2,1)}), bf16[128,2,16,128]{3,2,1,0:T(8,128)(2,1)S(1)}, u32[]{:S(2)}, u32[]{:S(2)}) async-start(bf16[128,2,16,128]{3,2,1,0:T(8,128)(2,1)} %bitcast.3), calls=%async_computation | async-start | bytes 2097152 | tf_op jit(solution)/shard_map/all_to_all | solution.py:343
  14.3 0.9 copy-start.4
  14.3 1.6 %copy-start.2 = (s32[16384]{0:T(1024)S(1)}, s32[16384]{0:T(1024)}, u32[]{:S(2)}) copy-start(s32[16384]{0:T(1024)} %param.7) | copy-start | bytes 196612
  32.1 1.0 %copy-start.1 = (bf16[128,2,16,128]{3,2,1,0:T(8,128)(2,1)}, bf16[128,2,16,128]{3,2,1,0:T(8,128)(2,1)S(1)}, u32[]{:S(2)}) copy-start(bf16[128,2,16,128]{3,2,1,0:T(8,128)(2,1)S(1)} %all-to-all-done) | copy-start | bytes 3145732
where the time goes:
time: 93.4 us; the launch traced here: 93.1 us
  Pallas kernels  58.4 us (63%)
  waiting for transfers between devices  15.2 us (16%)
  starting transfers between devices  10.8 us (12%)
  local copies, waits for them, and re-layouts  6.66 us (7%)
  other arithmetic  1.93 us (2%)
    pallas_call x1, Pallas kernels, shards(): pl.pallas_call(functools.partial(deblur_kernel, devices_x, devices_y, pla...  58.4 us
    all_to_all x1, waiting for transfers between devices, exchange(): lax.all_to_all(outgoing, ('gx', 'gy'), split_axis=0, concat_axis=0, tiled...  15.2 us
    all_to_all x1, starting transfers between devices, exchange(): lax.all_to_all(outgoing, ('gx', 'gy'), split_axis=0, concat_axis=0, tiled...  10.8 us
    unnamed x13, local copies, waits for them, and re-layouts  3.74 us
  transfers between devices with their start and end apart: 1, of which 1 were waited for; matrix products, arithmetic and copies ran while one was open for 3% of the time, Pallas kernels for 0%

commit v1 on v0

--- a/solution.py
+++ b/solution.py
@@ -27,10 +27,10 @@
 
 def deblur_kernel(
     devices_x, devices_y, planes, ext_x, views,
-    est_ref, arrived_ref, rows_ref, kidx_ref, psf_ref, out_ref,
+    est_ref, planes_ref, rows_ref, kidx_ref, psf_ref, out_ref,
     table, kz_small, kx_small, kz_wide, kx_wide, wy, kf, kt,
-    cur, cbuf, zcat, blur, rim, rim_send, rim_recv, qext, q_send, q_recv, u, part, part_recv, meas,
-    send_sem, recv_sem,
+    cur, cbuf, zcat, blur, rim, rim_send, rim_recv, qext, q_send, q_recv, u, part, part_recv, meas, arrived,
+    send_sem, recv_sem, plane_send_sem, plane_recv_sem,
 ):
     zx = planes * ext_x
     ny = est_ref.shape[1]
@@ -54,11 +54,20 @@
     slot_of = {"left": 0, "right": 1, "down": 0, "up": 1}
     back = {"left": "right", "right": "left", "down": "up", "up": "down"}
 
+    devices = devices_x * devices_y
+    me = gx * devices_y + gy
+
+    def partner(k):
+        other = lax.rem(me + k, devices)
+        return other, (other // devices_y, lax.rem(other, devices_y))
+
     barrier = pltpu.get_barrier_semaphore()
-    for side in has:
-        @pl.when(has[side])
-        def _(side=side):
-            pl.semaphore_signal(barrier, inc=1, device_id=to[side], device_id_type=MESH)
+
+    def greet(k, carry):
+        pl.semaphore_signal(barrier, inc=1, device_id=partner(k)[1], device_id_type=MESH)
+        return carry
+
+    lax.fori_loop(1, devices, greet, 0)
 
     def send(side, kind, src, dst):
         num = kind * 2 + slot_of[side]
@@ -106,14 +115,26 @@
             clear_missing("up", kind_buf.at[it, 1])
         clear_missing("left", part_recv.at[it, 0])
         clear_missing("right", part_recv.at[it, 1])
-    peers = sum(present.astype(jnp.int32) for present in has.values())
-    pl.semaphore_wait(barrier, peers)
 
     def send_current(it):
         send("left", 4 * it, cbuf.at[it, 1], cbuf.at[it, 2])
         send("right", 4 * it, cbuf.at[it, 1], cbuf.at[it, 0])
 
-    send_current(0)
+    def send_planes(k, carry):
+        other, where = partner(k)
+        pltpu.make_async_remote_copy(
+            src_ref=planes_ref.at[other], dst_ref=arrived.at[k],
+            send_sem=plane_send_sem, recv_sem=plane_recv_sem,
+            device_id=where, device_id_type=MESH,
+        ).start()
+        return carry
+
+    def all_planes():
+        return pltpu.make_async_remote_copy(
+            src_ref=arrived.at[pl.ds(1, devices - 1)], dst_ref=arrived.at[pl.ds(1, devices - 1)],
+            send_sem=plane_send_sem, recv_sem=plane_recv_sem,
+            device_id=partner(1)[1], device_id_type=MESH,
+        )
 
     weights = psf_ref[...]
     weights = weights / jnp.sum(weights, axis=1, keepdims=True)
@@ -165,6 +186,11 @@
                 edge = pltpu.roll(edge, 32 * v, 1)
             wy[v, i * ny:(i + 1) * ny, 128:256] = edge.astype(BF16)
 
+    pl.semaphore_wait(barrier, devices - 1)
+    send_current(0)
+    lax.fori_loop(1, devices, send_planes, 0)
+    arrived[0] = planes_ref[me]
+
     wide = (128, zx)
     row = iota(wide, 0)
     col = iota(wide, 1)
@@ -270,8 +296,12 @@
         if it == 0:
             build(1)
 
+            all_planes().wait_recv()
+
             def take(p, carry):
-                meas[pl.ds(pl.multiple_of(p * ext_x, ext_x), ext_x), :] = arrived_ref[rows_ref[p]]
+                place = rows_ref[p]
+                at = pl.ds(pl.multiple_of(p * ext_x, ext_x), ext_x)
+                meas[at, :] = arrived[place // 2, lax.rem(place, 2)]
                 return carry
 
             lax.fori_loop(0, views * planes, take, 0)
@@ -319,6 +349,7 @@
         else:
             out_ref[...] = updated
 
+    all_planes().wait_send()
     for it in range(ITERS):
         kind_c, kind_rim, kind_q, kind_p = (4 * it + k for k in range(4))
         for side in ("left", "right"):
@@ -340,7 +371,6 @@
     source = jnp.stack([first, last], axis=1).reshape(-1)
     outgoing = jnp.take(stored, source, axis=0, mode="clip")
     outgoing = outgoing.reshape((devices, 2) + stored.shape[1:])
-    arrived = lax.all_to_all(outgoing, ("gx", "gy"), split_axis=0, concat_axis=0, tiled=True)
     everything = placement.reshape(devices, slots)
     wanted = everything // slots == me
     item = everything % slots
@@ -349,13 +379,13 @@
     item_first = jnp.max(jnp.where(slot == first, item, -1), axis=1)
     item_last = jnp.max(jnp.where((slot == last) & (last > first), item, -1), axis=1)
     items = jnp.arange(slots, dtype=jnp.int32)[:, None]
-    origin = jnp.arange(devices, dtype=jnp.int32)[None, :]
+    origin = (me - jnp.arange(devices, dtype=jnp.int32)[None, :]) % devices
     row = jnp.max(
         jnp.where(item_first[None, :] == items, 2 * origin, 0)
         + jnp.where(item_last[None, :] == items, 2 * origin + 1, 0),
         axis=1,
     )
-    return arrived.reshape((2 * devices,) + stored.shape[1:]), row
+    return outgoing, row
 
 
 def solution(mesh):
@@ -365,7 +395,7 @@
         planes, ext_x, ny = estimate.shape
         zx = planes * ext_x
         views = kernel_index.shape[2]
-        arrived, row = exchange(stored, placement, devices_x * devices_y)
+        outgoing, row = exchange(stored, placement, devices_x * devices_y)
         vmem = pl.BlockSpec(memory_space=pltpu.VMEM)
         smem = pl.BlockSpec(memory_space=pltpu.SMEM)
         n = 3 * views
@@ -398,15 +428,18 @@
                 pltpu.VMEM((ITERS, 2, zx, ny), F32),
                 pltpu.VMEM((ITERS, 2, zx, ny), F32),
                 pltpu.VMEM((views * zx, ny), BF16),
+                pltpu.VMEM(outgoing.shape, BF16),
                 pltpu.SemaphoreType.DMA((8 * ITERS,)),
                 pltpu.SemaphoreType.DMA((8 * ITERS,)),
+                pltpu.SemaphoreType.DMA,
+                pltpu.SemaphoreType.DMA,
             ],
             compiler_params=pltpu.CompilerParams(
                 collective_id=0, has_side_effects=True, vmem_limit_bytes=60 * 1024 * 1024
             ),
         )(
             estimate.reshape(zx, ny),
-            arrived,
+            outgoing,
             row,
             kernel_index.reshape(-1),
             psf_taps,

time: 93.4 us -> 92.2 us (0.987)
  the two profiles are of different devices: /device:TPU:3 before, /device:TPU:34 now
where the time goes in v1:
time: 92.2 us; the launch traced here: 91.9 us
  Pallas kernels  82.8 us (90%)
  local copies, waits for them, and re-layouts  6.3 us (7%)
  other arithmetic  2.8 us (3%)
    pallas_call x1, Pallas kernels, shards(): pl.pallas_call(functools.partial(deblur_kernel, devices_x, devices_y, pla...  82.8 us
    unnamed x11, local copies, waits for them, and re-layouts  3.39 us

profile of v1, /device:TPU:34, one launch (start us, length us, event | category | flops | bytes accessed | tf_op | source)
XLA Modules:
  0.0 91.9 jit_solution(10927528028255770964)
XLA Ops:
  0.0 0.0 copy-start
  0.0 0.0 copy-start.1
  0.0 0.8 and_select_fusion.1
  0.8 0.1 select_reduce_fusion.5
  1.0 1.0 %select_reduce_fusion.3 = (s32[128]{0:T(128)S(1)}, s32[128]{0:T(128)S(1)}) fusion(s32[]{:T(128)S(6)} %add.40, s32[16384]{0:T(1024)} %param.7), kind=kLoop, calls=%fused_computation.17 | loop fusion | flops 327424 | bytes 66564 | tf_op jit(solution)/shard_map/reduce_min | solution.py:377
  2.0 0.0 copy-done.1
  2.0 0.0 copy-start.3
  2.0 0.2 select_reduce_fusion.2
  2.2 0.6 add_reduce_fusion.rows_ref
  2.8 0.0 copy-done.3
  2.8 0.7 copy.12.psf_ref
  3.5 0.1 copy.10
  3.6 0.0 copy-start.2
  3.6 0.1 reshape.62
  3.8 0.6 copy-done.2
  4.4 0.4 copy.11
  4.8 0.9 reshape.58.kidx_ref
  5.7 0.0 copy-done
  5.7 1.8 %gather_fusion = bf16[256,16,128]{2,1,0:T(8,128)(2,1)} fusion(bf16[128,16,128]{2,1,0:T(8,128)(2,1)S(1)} %copy-done, s32[1024]{0:T(1024)S(1)} %pad_clamp_fusion), kind=kCustom, calls=%fused_computation | custom fusion | bytes 2098176 | tf_op jit(solution)/shard_map/jit(_take)/gather | solution.py:372
  7.5 82.8 %shard_map.55 = f32[512,128]{1,0:T(8,128)} custom-call(f32[512,128]{1,0:T(8,128)} %bitcast.37, bf16[128,2,16,128]{3,2,1,0:T(8,128)(2,1)} %bitcast.35, s32[128]{0:T(128)} %add_reduce_fusion.rows_ref, s32[1536]{0:T(1024)} %reshape.58.kidx_ref, f32[48,31]{1,0:T(8,128)} %copy.12.psf_ref), custom_call_target="tpu_custom_call" | custom-call | tf_op jit(solution)/shard_map/pallas_call | solution.py:403
  90.3 1.7 %copy.14 = f32[32,16,128]{2,1,0:T(8,128)} copy(f32[32,16,128]{2,1,0:T(8,128)} %bitcast.36) | data formatting | bytes 524288
  (4 shorter events, 0.0 us)
Async XLA Ops:
  0.0 5.7 %copy-start = (bf16[128,16,128]{2,1,0:T(8,128)(2,1)S(1)}, bf16[128,16,128]{2,1,0:T(8,128)(2,1)}, u32[]{:S(2)}) copy-start(bf16[128,16,128]{2,1,0:T(8,128)(2,1)} %param.6) | copy-start | bytes 1572868
  0.0 2.0 %copy-start.1 = (s32[16384]{0:T(1024)S(1)}, s32[16384]{0:T(1024)}, u32[]{:S(2)}) copy-start(s32[16384]{0:T(1024)} %param.7) | copy-start | bytes 196612
  2.0 0.9 copy-start.3
  3.6 0.8 copy-start.2

commit v2 on v1

--- a/solution.py
+++ b/solution.py
@@ -120,14 +120,22 @@
         send("left", 4 * it, cbuf.at[it, 1], cbuf.at[it, 2])
         send("right", 4 * it, cbuf.at[it, 1], cbuf.at[it, 0])
 
-    def send_planes(k, carry):
-        other, where = partner(k)
-        pltpu.make_async_remote_copy(
-            src_ref=planes_ref.at[other], dst_ref=arrived.at[k],
-            send_sem=plane_send_sem, recv_sem=plane_recv_sem,
-            device_id=where, device_id_type=MESH,
-        ).start()
-        return carry
+    stride = next(s for s in (37, 41, 43, 47) if devices % s)
+    share = -(-(devices - 1) // (6 * views))
+
+    def send_planes(step):
+        for j in range(share):
+            turn = step * share + j + 1
+
+            @pl.when(turn < devices)
+            def _(turn=turn):
+                k = lax.rem(turn * stride, devices)
+                other, where = partner(k)
+                pltpu.make_async_remote_copy(
+                    src_ref=planes_ref.at[other], dst_ref=arrived.at[k],
+                    send_sem=plane_send_sem, recv_sem=plane_recv_sem,
+                    device_id=where, device_id_type=MESH,
+                ).start()
 
     def all_planes():
         return pltpu.make_async_remote_copy(
@@ -188,7 +196,6 @@
 
     pl.semaphore_wait(barrier, devices - 1)
     send_current(0)
-    lax.fori_loop(1, devices, send_planes, 0)
     arrived[0] = planes_ref[me]
 
     wide = (128, zx)
@@ -211,6 +218,8 @@
 
     def build(way):
         def one(n, carry):
+            if way == 0:
+                send_planes(n)
             i = n // views
             v = lax.rem(n, views)
             num = way * 3 * views + n
@@ -248,6 +257,8 @@
 
     def forward_zx(it, i):
         def one(v, carry):
+            if it == 0:
+                send_planes((3 + (1, 0, 2)[i]) * views + v)
             at = pl.multiple_of(v * zx, zx)
             zcat[pl.ds(at, zx), i * ny:(i + 1) * ny] = dot(
                 kf[i, pl.ds(at, zx), :], cbuf[it, i]

time: 92.2 us -> 84.7 us (0.919)
  Pallas kernels: 82.8 us -> 74.8 us
    pallas_call x1, Pallas kernels: 82.8 us -> 74.8 us  [shards(): pl.pallas_call(functools.partial(deblur_kernel, devices_x, devices_y, pla...]
where the time goes in v2:
time: 84.7 us; the launch traced here: 84 us
  Pallas kernels  74.8 us (88%)
  local copies, waits for them, and re-layouts  6.3 us (7%)
  other arithmetic  2.8 us (3%)
    pallas_call x1, Pallas kernels, shards(): pl.pallas_call(functools.partial(deblur_kernel, devices_x, devices_y, pla...  74.8 us
    unnamed x11, local copies, waits for them, and re-layouts  3.39 us
    gather x1, local copies, waits for them, and re-layouts, exchange(): outgoing = jnp.take(stored, source, axis=0, mode='clip')  1.77 us

profile of v2, /device:TPU:34, one launch (start us, length us, event | category | flops | bytes accessed | tf_op | source)
XLA Modules:
  0.0 84.0 jit_solution(206415958151617914)
XLA Ops:
  0.0 0.0 copy-start
  0.0 0.0 copy-start.1
  0.0 0.8 and_select_fusion.1
  0.8 0.1 select_reduce_fusion.5
  1.0 1.0 %select_reduce_fusion.3 = (s32[128]{0:T(128)S(1)}, s32[128]{0:T(128)S(1)}) fusion(s32[]{:T(128)S(6)} %add.40, s32[16384]{0:T(1024)} %param.7), kind=kLoop, calls=%fused_computation.17 | loop fusion | flops 327424 | bytes 66564 | tf_op jit(solution)/shard_map/reduce_min | solution.py:388
  2.0 0.0 copy-done.1
  2.0 0.0 copy-start.3
  2.0 0.2 select_reduce_fusion.2
  2.2 0.6 add_reduce_fusion.rows_ref
  2.8 0.0 copy-done.3
  2.8 0.7 copy.12.psf_ref
  3.5 0.1 copy.10
  3.6 0.0 copy-start.2
  3.6 0.1 reshape.62
  3.8 0.6 copy-done.2
  4.4 0.4 copy.11
  4.8 0.9 %reshape.58.kidx_ref = s32[1536]{0:T(1024)} reshape(s32[16,8,4,3]{3,2,1,0:T(4,128)S(1)} %copy.11) | data formatting | bytes 12288 | tf_op jit(solution)/shard_map/reshape | solution.py:455
  5.7 0.0 copy-done
  5.7 1.8 %gather_fusion = bf16[256,16,128]{2,1,0:T(8,128)(2,1)} fusion(bf16[128,16,128]{2,1,0:T(8,128)(2,1)S(1)} %copy-done, s32[1024]{0:T(1024)S(1)} %pad_clamp_fusion), kind=kCustom, calls=%fused_computation | custom fusion | bytes 2098176 | tf_op jit(solution)/shard_map/jit(_take)/gather | solution.py:383
  7.5 74.8 %shard_map.55 = f32[512,128]{1,0:T(8,128)} custom-call(f32[512,128]{1,0:T(8,128)} %bitcast.37, bf16[128,2,16,128]{3,2,1,0:T(8,128)(2,1)} %bitcast.35, s32[128]{0:T(128)} %add_reduce_fusion.rows_ref, s32[1536]{0:T(1024)} %reshape.58.kidx_ref, f32[48,31]{1,0:T(8,128)} %copy.12.psf_ref), custom_call_target="tpu_custom_call" | custom-call | tf_op jit(solution)/shard_map/pallas_call | solution.py:414
  82.3 1.7 %copy.14 = f32[32,16,128]{2,1,0:T(8,128)} copy(f32[32,16,128]{2,1,0:T(8,128)} %bitcast.36) | data formatting | bytes 524288
  (4 shorter events, 0.0 us)
Async XLA Ops:
  0.0 5.7 %copy-start = (bf16[128,16,128]{2,1,0:T(8,128)(2,1)S(1)}, bf16[128,16,128]{2,1,0:T(8,128)(2,1)}, u32[]{:S(2)}) copy-start(bf16[128,16,128]{2,1,0:T(8,128)(2,1)} %param.6) | copy-start | bytes 1572868
  0.0 2.0 %copy-start.1 = (s32[16384]{0:T(1024)S(1)}, s32[16384]{0:T(1024)}, u32[]{:S(2)}) copy-start(s32[16384]{0:T(1024)} %param.7) | copy-start | bytes 196612
  2.0 0.9 %copy-start.3 = (f32[48,31]{0,1:T(8,128)S(1)}, f32[48,31]{0,1:T(8,128)}, u32[]{:S(2)}) copy-start(f32[48,31]{0,1:T(8,128)} %param.8) | copy-start | bytes 17860
  3.6 0.8 copy-start.2
